TPU v7x, 32 devices: a whole 2x2x4 slice. The times are simulated.
32 devices in a mesh: tok: 2 (over x), feat: 4 (over z), pb: 4 (over y, core).
Axes of the slice: x: 2, y: 2, z: 4, core: 2. Of those that a mesh axis runs over, the one named last changes fastest.
Arguments:
- out_grads: bfloat16 [10240, 8192], P(('tok', 'pb'), 'feat'), may hold values from -6 to 6
- acts: bfloat16 [10240, 8192], P(('tok', 'pb'), 'feat'), may hold values from -6 to 6
- s_inverse: bfloat16 [8192, 8192], P('feat', ('tok', 'pb')), may hold values from -1 to 3, as said below
- a_inverse: bfloat16 [8192, 8192], P('feat', ('tok', 'pb')), may hold values from -1 to 3, as said below
- query_out: bfloat16 [8192, 512], P(('tok', 'pb')), may hold values from -0.0625 to 0.0625
- query_in: bfloat16 [8192, 512], P(('tok', 'pb')), may hold values from -0.0625 to 0.0625
Outputs:
- scores: float32 [32, 10240], P('feat', ('tok', 'pb'))
Inputs may be any that keep to these rules, and one draw needn't show every extreme that they name: `s_inverse`: symmetric; diagonal entries roughly between 0.5 and 2. `a_inverse`: symmetric; diagonal entries roughly between 0.5 and 2.
All inputs are finite; a program needn't handle non-finite values.
Results may differ from a plain program's by a relative error of at most 0.0041.
Values may be sent and summed in bfloat16 or wider, within the bound.
No kernel may reach another device: no remote copies, remote signals or barrier semaphores. Data moves between devices by JAX's collectives and lax.ppermute only.
A program may use at most 128 MiB of HBM per device.

v0:
```python
import jax
import jax.numpy as jnp
from jax import lax
from jax.sharding import PartitionSpec as P

RANK = 16


def per_device(out_grads, acts, s_inverse, a_inverse, query_out, query_in):
    left_part = jnp.dot(s_inverse, query_out, preferred_element_type=jnp.float32)
    right_part = jnp.dot(a_inverse, query_in, preferred_element_type=jnp.float32)
    left_rows, right_rows = (
        lax.psum_scatter(left_part, ("tok", "pb"), scatter_dimension=0, tiled=True),
        lax.psum_scatter(right_part, ("tok", "pb"), scatter_dimension=0, tiled=True),
    )
    left_rows = left_rows.astype(jnp.bfloat16)
    right_rows = right_rows.astype(jnp.bfloat16)
    token_rows = out_grads.shape[0]
    width = left_rows.shape[1]
    left_block, right_block = (
        lax.all_gather(left_rows, ("tok", "pb"), axis=0, tiled=True),
        lax.all_gather(right_rows, ("tok", "pb"), axis=0, tiled=True),
    )
    grad_part = jnp.dot(out_grads, left_block, preferred_element_type=jnp.float32)
    act_part = jnp.dot(acts, right_block, preferred_element_type=jnp.float32)
    feat_count = lax.axis_size("feat")
    share = width // feat_count
    grad_proj, act_proj = (
        lax.psum_scatter(grad_part, "feat", scatter_dimension=1, tiled=True),
        lax.psum_scatter(act_part, "feat", scatter_dimension=1, tiled=True),
    )
    scale = 1.0 / RANK**0.5
    summed = (grad_proj * act_proj).reshape(token_rows, share // RANK, RANK).sum(axis=2)
    return (summed * scale).T


def solution(mesh):
    placed = (
        P(("tok", "pb"), "feat"),
        P(("tok", "pb"), "feat"),
        P("feat", ("tok", "pb")),
        P("feat", ("tok", "pb")),
        P(("tok", "pb"), None),
        P(("tok", "pb"), None),
    )
    return jax.shard_map(
        per_device, mesh=mesh, in_specs=placed, out_specs=P("feat", ("tok", "pb")), check_vma=False
    )
```

profile of v0, /device:TPU:0, one launch (start us, length us, event | category | flops | bytes accessed | tf_op | source)
XLA Modules:
  0.0 299.4 jit_solution(6512004176010741988)
XLA Ops:
  6.5 0.0 copy-start
  6.5 0.0 reduce-scatter.5.cloned.1.call-start
  6.5 1.2 copy-done
  7.8 6.5 %fusion = f32[2048,512]{1,0:T(8,128)} fusion(bf16[2048,1024]{1,0:T(8,128)(2,1)} %param.8, bf16[1024,512]{1,0:T(8,128)(2,1)S(1)} %copy-done), kind=kOutput, calls=%fused_computation.4 | convolution fusion | flops 2147483648 | bytes 9437184 | tf_op jit(solution)/shard_map/dot_general | solution.py:10
  14.3 0.0 copy-start.1
  14.3 0.0 reduce-scatter.5.cloned.1.call-update
  14.3 0.0 reduce-scatter.9.cloned.1.call-start
  14.3 1.1 copy-done.1
  15.5 6.5 %fusion.1 = f32[2048,512]{1,0:T(8,128)} fusion(bf16[2048,1024]{1,0:T(8,128)(2,1)} %param.9, bf16[1024,512]{1,0:T(8,128)(2,1)S(1)} %copy-done.1), kind=kOutput, calls=%fused_computation.5 | convolution fusion | flops 2147483648 | bytes 9437184 | tf_op jit(solution)/shard_map/dot_general | solution.py:11
  21.9 0.0 reduce-scatter.9.cloned.1.call-update
  22.0 0.0 all-gather.3.cloned.1.call-start
  22.0 46.3 %reduce-scatter.5.cloned.1.call-done = f32[256,512]{1,0:T(8,128)} async-done(((f32[2048,512]{1,0:T(8,128)}), f32[256,512]{1,0:T(8,128)}) %reduce-scatter.5.cloned.1.call-update) | async-done | bytes 524304 | tf_op jit(solution)/shard_map/reduce_scatter | solution.py:13
  68.3 1.8 convert_element_type.6
  70.1 0.0 all-gather.3.cloned.1.call-update
  70.1 0.0 all-gather.5.cloned.1.call-start
  70.2 52.7 %reduce-scatter.9.cloned.1.call-done = f32[256,512]{1,0:T(8,128)} async-done(((f32[2048,512]{1,0:T(8,128)}), f32[256,512]{1,0:T(8,128)}) %reduce-scatter.9.cloned.1.call-update) | async-done | bytes 524304 | tf_op jit(solution)/shard_map/reduce_scatter | solution.py:14
  122.9 1.8 convert_element_type.7
  124.7 0.0 all-gather.5.cloned.1.call-update
  124.7 0.0 reduce-scatter.7.cloned.1.call-start
  124.7 27.8 %all-gather.3.cloned.1.call-done = bf16[2048,512]{1,0:T(8,128)(2,1)} async-done(((bf16[256,512]{1,0:T(8,128)(2,1)}), bf16[2048,512]{1,0:T(8,128)(2,1)}) %all-gather.3.cloned.1.call-update) | async-done | bytes 2097168 | tf_op jit(solution)/shard_map/all_gather | solution.py:21
  152.5 7.6 %convolution_bitcast_fusion.1 = f32[1280,512]{0,1:T(8,128)} fusion(bf16[2048,512]{1,0:T(8,128)(2,1)} %all-gather.3.cloned.1.call-done, bf16[1280,2048]{1,0:T(8,128)(2,1)} %param.6), kind=kOutput, calls=%fused_computation.1 | convolution fusion | flops 2684354560 | bytes 9961472 | tf_op jit(solution)/shard_map/dot_general | solution.py:24
  160.1 0.0 reduce-scatter.7.cloned.1.call-update
  160.1 0.0 reduce-scatter.11.cloned.1.call-start
  160.2 21.9 %all-gather.5.cloned.1.call-done = bf16[2048,512]{1,0:T(8,128)(2,1)} async-done(((bf16[256,512]{1,0:T(8,128)(2,1)}), bf16[2048,512]{1,0:T(8,128)(2,1)}) %all-gather.5.cloned.1.call-update) | async-done | bytes 2097168 | tf_op jit(solution)/shard_map/all_gather | solution.py:22
  182.1 7.5 %convolution_bitcast_fusion = f32[1280,512]{0,1:T(8,128)} fusion(bf16[2048,512]{1,0:T(8,128)(2,1)} %all-gather.5.cloned.1.call-done, bf16[1280,2048]{1,0:T(8,128)(2,1)} %param.7), kind=kOutput, calls=%fused_computation | convolution fusion | flops 2684354560 | bytes 9961472 | tf_op jit(solution)/shard_map/dot_general | solution.py:25
  189.6 0.0 reduce-scatter.11.cloned.1.call-update
  189.7 46.9 %reduce-scatter.7.cloned.1.call-done = f32[1280,128]{0,1:T(8,128)} async-done(((f32[1280,512]{0,1:T(8,128)}), f32[1280,128]{0,1:T(8,128)}) %reduce-scatter.7.cloned.1.call-update) | async-done | bytes 655376 | tf_op jit(solution)/shard_map/reduce_scatter | solution.py:29
  236.5 54.0 %reduce-scatter.11.cloned.1.call-done = f32[1280,128]{0,1:T(8,128)} async-done(((f32[1280,512]{0,1:T(8,128)}), f32[1280,128]{0,1:T(8,128)}) %reduce-scatter.11.cloned.1.call-update) | async-done | bytes 655376 | tf_op jit(solution)/shard_map/reduce_scatter | solution.py:30
  290.6 1.4 bitcast_reduce_fusion
  292.0 0.6 multiply_bitcast_fusion
Async XLA Ops:
  6.5 1.2 copy-start
  6.5 61.8 %reduce-scatter.5.cloned.1.call-start = ((), (), s32[]{:S(2)}) async-start(), calls=%async_computation.4 | async-start | bytes 4718592 | tf_op jit(solution)/shard_map/reduce_scatter | solution.py:13
  14.3 1.2 copy-start.1
  14.3 108.6 %reduce-scatter.9.cloned.1.call-start = ((), (), s32[]{:S(2)}) async-start(), calls=%async_computation.7 | async-start | bytes 4718592 | tf_op jit(solution)/shard_map/reduce_scatter | solution.py:14
  22.0 130.6 %all-gather.3.cloned.1.call-start = ((), (), s32[]{:S(2)}) async-start(), calls=%async_computation.5 | async-start | bytes 2359296 | tf_op jit(solution)/shard_map/all_gather | solution.py:21
  70.1 112.0 %all-gather.5.cloned.1.call-start = ((), (), s32[]{:S(2)}) async-start(), calls=%async_computation.8 | async-start | bytes 2359296 | tf_op jit(solution)/shard_map/all_gather | solution.py:22
  124.7 111.9 %reduce-scatter.7.cloned.1.call-start = ((), (), s32[]{:S(2)}) async-start(), calls=%async_computation.6 | async-start | bytes 3276800 | tf_op jit(solution)/shard_map/reduce_scatter | solution.py:29
  160.1 130.4 %reduce-scatter.11.cloned.1.call-start = ((), (), s32[]{:S(2)}) async-start(), calls=%async_computation.9 | async-start | bytes 3276800 | tf_op jit(solution)/shard_map/reduce_scatter | solution.py:30
Sparse Core Ops, SparseCore 0:
  14.4 53.8 reduce-scatter.4
  71.7 51.1 reduce-scatter.8
  124.8 27.7 all-gather.2
  154.3 27.7 all-gather.4
  184.2 52.2 reduce-scatter.6
  238.7 51.8 reduce-scatter.10
where the time goes:
time: 300 us; the launch traced here: 299 us
  waiting for transfers between devices  250 us (83%)
  matrix products  28.1 us (9%)
  between operations  13.5 us (4%)
  other arithmetic  5.6 us (2%)
    reduce_scatter x1, waiting for transfers between devices, per_device(): lax.psum_scatter(act_part, 'feat', scatter_dimension=1, tiled=True)  54 us
    reduce_scatter x1, waiting for transfers between devices, per_device(): lax.psum_scatter(right_part, ('tok', 'pb'), scatter_dimension=0, tiled=True)  52.7 us
    reduce_scatter x1, waiting for transfers between devices, per_device(): lax.psum_scatter(grad_part, 'feat', scatter_dimension=1, tiled=True)  46.9 us
    reduce_scatter x1, waiting for transfers between devices, per_device(): lax.psum_scatter(left_part, ('tok', 'pb'), scatter_dimension=0, tiled=True)  46.3 us
    all_gather x1, waiting for transfers between devices, per_device(): lax.all_gather(left_rows, ('tok', 'pb'), axis=0, tiled=True)  27.8 us
    all_gather x1, waiting for transfers between devices, per_device(): lax.all_gather(right_rows, ('tok', 'pb'), axis=0, tiled=True)  21.9 us
    dot_general x1, matrix products, per_device(): jnp.dot(out_grads, left_block, preferred_element_type=jnp.float32)  7.56 us
    dot_general x1, matrix products, per_device(): act_part = jnp.dot(acts, right_block, preferred_element_type=jnp.float32)  7.54 us
  transfers between devices with their start and end apart: 6, of which 6 were waited for; matrix products, arithmetic and copies ran while one was open for 8% of the time, Pallas kernels for 0%

commit v1 on v0

v1 whole, which is shorter than its diff:
```python
import functools

import jax
import jax.numpy as jnp
import numpy as np
from jax import lax
from jax.experimental import pallas as pl
from jax.experimental.pallas import tpu as pltpu
from jax.sharding import PartitionSpec as P


RANK = 16
SEND = jnp.float16
PAD = 8
F32 = jnp.float32
BF16 = jnp.bfloat16
GROUPS = ((3,), (2,), (1, 0))


def cost(flops, bytes_accessed):
    return pl.CostEstimate(flops=int(flops), bytes_accessed=int(bytes_accessed), transcendentals=0)


def factor_part(slots, scal, s_ref, a_ref, *rest):
    q_refs, rest, held = rest[: 2 * slots], rest[2 * slots : -1], rest[-1]
    share = q_refs[0].shape[1]
    for j, f_ref in enumerate((s_ref, a_ref)):

        @pl.when(pl.program_id(0) == j)
        def _(f_ref=f_ref, q_refs=q_refs[j * slots : (j + 1) * slots]):
            for i, q_ref in enumerate(q_refs):
                held[:, i * share : (i + 1) * share] = q_ref[...]
            value = jnp.dot(f_ref[...], held[...], preferred_element_type=F32)
            if len(rest) == 1:
                rest[0][0] = value
            else:
                spread(scal, value, *rest)


def spread(scal, value, got_ref, *rest):
    outs, total = rest[:-1], rest[-1]
    value += got_ref[0]
    top = jnp.max(jnp.abs(value), axis=(0, 1), keepdims=True) * (1.0 / 30000.0)
    root = jnp.sqrt(jnp.sqrt(jnp.maximum(top, 2.0**-52))).astype(BF16).astype(F32)
    scale = 1.0 / (root * root * root * root)
    total[...] = value
    rows = outs[0].shape[1]
    chips = value.shape[0] // rows
    at = 0
    for group in range(len(outs) // chips):
        cols = outs[group * chips].shape[2]
        for m in range(chips):
            out = outs[group * chips + m]
            share = total[pl.ds(pl.multiple_of((scal[1] ^ m) * rows, rows), rows), at : at + cols]
            if m:
                out[0, :rows] = share * scale
                out[0, rows:] = jnp.broadcast_to(root, (PAD, cols))
            else:
                out[0] = share
        at += cols


def factor_call(scal, factors, queries, got, keep, masks, rows, share, outs):
    depth = factors[0].shape[1]
    slots = len(masks)
    cols = slots * share
    half = lambda sc: sc[0] if keep else 1 - sc[0]
    in_specs = [pl.BlockSpec((rows, depth), lambda j, sc: (half(sc), 0))] * 2
    for _ in queries:
        for mask in masks:
            in_specs.append(pl.BlockSpec((depth, share), lambda j, sc, mask=mask: (0, sc[2] ^ mask)))
    operands = [*factors, *[q for q in queries for _ in masks]]
    scratch = [pltpu.VMEM((depth, cols), BF16)]
    if keep:
        in_specs.append(pl.BlockSpec((1, rows, cols), lambda j, sc: (j, 0, 0)))
        operands.append(got)
        scratch.insert(0, pltpu.VMEM((rows, cols), F32))
    return pl.pallas_call(
        functools.partial(factor_part, slots),
        out_shape=outs,
        grid_spec=pltpu.PrefetchScalarGridSpec(
            num_scalar_prefetch=1,
            grid=(2,),
            in_specs=in_specs,
            out_specs=[pl.BlockSpec((1, *o.shape[1:]), lambda j, sc: (j, 0, 0)) for o in outs],
            scratch_shapes=scratch,
        ),
        compiler_params=pltpu.CompilerParams(dimension_semantics=("arbitrary",), vmem_limit_bytes=24 << 20),
        cost_estimate=cost(4 * rows * depth * cols, 4 * rows * depth + 4 * depth * cols + 8 * rows * cols),
    )(scal, *operands)


def project(chips, scal, g_ref, a_ref, *rest):
    blocks, outs, held = rest[: 2 * chips], rest[2 * chips : -1], rest[-1]
    rows = blocks[0].shape[1]
    core, chip = scal[0], scal[1]

    @pl.when(pl.program_id(1) == 0)
    def _():
        for m in range(chips):
            at = (chip ^ m) * rows
            for half, block in ((core, blocks[m]), (1 - core, blocks[chips + m])):
                held[pl.ds(pl.multiple_of(half * (chips * rows) + at, rows), rows), :] = block[0]

    for j, tokens_ref in enumerate((g_ref, a_ref)):

        @pl.when(pl.program_id(0) == j)
        def _(tokens_ref=tokens_ref):
            value = jnp.dot(tokens_ref[...], held[...], preferred_element_type=F32)
            at = 0
            for out in outs:
                out[0] = value[:, at : at + out.shape[2]].astype(out.dtype)
                at += out.shape[2]


def tile_of(count):
    return count // 2 if count % 256 == 0 else count


def project_call(scal, tokens, blocks, share, out_types):
    count, feats = tokens[0].shape
    chips, (_, rows, cols) = len(blocks) // 2, blocks[0].shape
    tile = tile_of(count)
    steps = count // tile
    in_specs = [
        pl.BlockSpec((tile, feats), lambda j, t, sc: (jnp.where(j == 0, t, steps - 1), 0)),
        pl.BlockSpec((tile, feats), lambda j, t, sc: (jnp.where(j == 1, t, 0), 0)),
        *[pl.BlockSpec((1, rows, cols), lambda j, t, sc: (j, 0, 0)) for _ in blocks],
    ]
    return pl.pallas_call(
        functools.partial(project, chips),
        out_shape=[jax.ShapeDtypeStruct((2, count, share), t) for t in out_types],
        grid_spec=pltpu.PrefetchScalarGridSpec(
            num_scalar_prefetch=1,
            grid=(2, steps),
            in_specs=in_specs,
            out_specs=[pl.BlockSpec((1, tile, share), lambda j, t, sc: (j, t, 0)) for _ in out_types],
            scratch_shapes=[pltpu.VMEM((feats, cols), BF16)],
        ),
        compiler_params=pltpu.CompilerParams(dimension_semantics=("arbitrary", "arbitrary"), vmem_limit_bytes=24 << 20),
        cost_estimate=cost(4 * count * feats * cols, 4 * count * feats + 4 * feats * cols),
    )(scal, *tokens, *blocks)


def score(*refs):
    parts, out_ref = refs[:-1], refs[-1]
    grads, acts = (sum(p[j].astype(F32) for p in parts) for j in range(2))
    turned = (grads * acts).T
    out_ref[...] = turned.reshape(out_ref.shape[0], RANK, turned.shape[1]).sum(axis=1) * (1.0 / RANK**0.5)


def score_call(*parts):
    _, count, share = parts[0].shape
    tile = tile_of(count)
    return pl.pallas_call(
        score,
        out_shape=jax.ShapeDtypeStruct((share // RANK, count), F32),
        grid=(count // tile,),
        in_specs=[pl.BlockSpec((2, tile, share), lambda t: (0, t, 0))] * len(parts),
        out_specs=pl.BlockSpec((share // RANK, tile), lambda t: (0, t)),
        compiler_params=pltpu.CompilerParams(vmem_limit_bytes=24 << 20),
        cost_estimate=cost(16 * count * share, 16 * count * share),
    )(*parts)


def by_collectives(out_grads, acts, s_inverse, a_inverse, query_out, query_in):
    group = ("tok", "pb")
    projected = []
    for tokens, factor, query in ((out_grads, s_inverse, query_out), (acts, a_inverse, query_in)):
        part = jnp.dot(factor, query, preferred_element_type=F32)
        rows = lax.psum_scatter(part, group, scatter_dimension=0, tiled=True).astype(BF16)
        block = lax.all_gather(rows, group, axis=0, tiled=True)
        part = jnp.dot(tokens, block, preferred_element_type=F32)
        projected.append(lax.psum_scatter(part, "feat", scatter_dimension=1, tiled=True))
    count, share = projected[0].shape
    summed = (projected[0] * projected[1]).reshape(count, share // RANK, RANK).sum(axis=2)
    return (summed * (1.0 / RANK**0.5)).T


def by_transfers(out_grads, acts, s_inverse, a_inverse, query_out, query_in):
    group = ("tok", "pb")
    size, planes = lax.axis_size(group), lax.axis_size("feat")
    at, plane = lax.axis_index(group), lax.axis_index("feat")
    chips, rows, share = size // 2, s_inverse.shape[0] // size, query_out.shape[1] // planes
    table = np.asarray([(i % 2, i // 2, z) for i in range(size) for z in range(planes)], np.int32)
    scal = lax.dynamic_index_in_dim(jnp.asarray(table), at * planes + plane, keepdims=False)
    factors, queries, tokens = (s_inverse, a_inverse), (query_out, query_in), (out_grads, acts)
    half = chips * rows

    def swap(v, m):
        return lax.ppermute(v, group, [(i, i ^ m) for i in range(size)])

    def hop(v, pairs):
        return lax.ppermute(v, "feat", pairs)

    def sent(masks):
        out = jax.ShapeDtypeStruct((2, half, len(masks) * share), F32)
        return factor_call(scal, factors, queries, None, False, masks, half, share, [out])[0]

    def kept(got, groups):
        masks = sum(groups, ())
        outs = [
            jax.ShapeDtypeStruct((2, rows + (PAD if m else 0), len(g) * share), F32) for g in groups for m in range(chips)
        ]
        outs = factor_call(scal, factors, queries, got, True, masks, half, share, outs)
        return [outs[i * chips : (i + 1) * chips] for i in range(len(groups))]

    def reduced(parts):
        total = parts[0]
        for m in range(1, chips):
            got = swap(parts[m].astype(SEND), 2 * m).astype(F32)
            total = total + got[:, :rows] * got[:, rows : rows + 1] ** 4
        return total.astype(BF16)

    def gathered(total):
        mine = [total, *[swap(total, 2 * m) for m in range(1, chips)]]
        return [*mine, *[swap(v, 1) for v in mine]]

    def projected(blocks, types):
        return project_call(scal, tokens, blocks, share, types)

    first, second, third = GROUPS
    sent_ab = sent(first + second)
    got_ab = swap(sent_ab, 1)
    sent_c = sent(third)
    got_c = swap(sent_c, 1)
    parts_a, parts_b = kept(got_ab, (first, second))
    (parts_c,) = kept(got_c, (third,))
    blocks_a = gathered(reduced(parts_a))
    blocks_b = gathered(reduced(parts_b))
    blocks_c = gathered(reduced(parts_c))

    (near,) = projected(blocks_a, (BF16,))
    right = hop(near, [(0, 1), (1, 2)])
    left = hop(near, [(3, 2), (2, 1)])
    (far,) = projected(blocks_b, (F32,))
    on_right, on_left = jnp.where(plane == 1, right, 0), jnp.where(plane == 2, left, 0)
    far = (far + on_right.astype(F32) + on_left.astype(F32)).astype(BF16)
    far = hop(far, [(0, 2), (1, 3), (2, 0), (3, 1)])
    mine = jnp.where(plane == 1, left, 0) + jnp.where(plane == 2, right, 0)
    side, own = projected(blocks_c, (BF16, F32))
    side = hop(side, [(0, 1), (1, 0), (2, 3), (3, 2)])
    return score_call(own, mine, side, far)


def solution(mesh):
    placed = (
        P(("tok", "pb"), "feat"),
        P(("tok", "pb"), "feat"),
        P("feat", ("tok", "pb")),
        P("feat", ("tok", "pb")),
        P(("tok", "pb"), None),
        P(("tok", "pb"), None),
    )

    chips, planes = mesh.shape["tok"] * mesh.shape["pb"] // 2, mesh.shape["feat"]
    direct = chips == 4 and planes == 4

    def per_device(*args):
        return by_transfers(*args) if direct else by_collectives(*args)

    return jax.shard_map(
        per_device, mesh=mesh, in_specs=placed, out_specs=P("feat", ("tok", "pb")), check_vma=False
    )
```

time: 300 us -> 125 us (0.42)
  waiting for transfers between devices: 250 us -> 45.2 us
  starting transfers between devices: 0.21 us -> 37.6 us
  matrix products: 28.1 us -> 0 us
  Pallas kernels: 0 us -> 24.2 us
  local copies, waits for them, and re-layouts: 2.37 us -> 15.6 us
  between operations: 13.5 us -> 0.46 us
  other arithmetic: 5.6 us -> 1.27 us
    reduce_scatter x4 -> x0, waiting for transfers between devices: 200 us -> none  [the longest x1 54 us: per_device(): lax.psum_scatter(act_part, 'feat', scatter_dimension=1, tiled=True)]
    all_gather x2 -> x0, waiting for transfers between devices: 49.7 us -> none  [the longest x1 27.8 us: per_device(): lax.all_gather(left_rows, ('tok', 'pb'), axis=0, tiled=True)]
    ppermute x0 -> x36, waiting for transfers between devices: none -> 45.2 us  [the longest x4 29.3 us: hop(): return lax.ppermute(v, 'feat', pairs)]
    ppermute x0 -> x36, starting transfers between devices: none -> 37.6 us  [the longest x32 27.5 us: swap(): return lax.ppermute(v, group, [(i, i ^ m) for i in range(size)])]
    dot_general x4 -> x0, matrix products: 28.1 us -> none  [the longest x1 7.56 us: per_device(): jnp.dot(out_grads, left_block, preferred_element_type=jnp.float32)]
    pallas_call x0 -> x8, Pallas kernels: none -> 24.2 us  [the longest x3 12.6 us: project_call(): pl.pallas_call(functools.partial(project, chips), out_shape=[jax.ShapeDty...]
    unnamed x4 -> x31, local copies, waits for them, and re-layouts: 2.37 us -> 14.9 us
  transfers between devices with their start and end apart: 6 -> 36, of which waited for: 6 -> 9; matrix products, arithmetic and copies ran while one was open for 8% -> 1% of each run, Pallas kernels for 0% -> 17%
where the time goes in v1:
time: 125 us; the launch traced here: 124 us
  waiting for transfers between devices  45.2 us (36%)
  starting transfers between devices  37.6 us (30%)
  Pallas kernels  24.2 us (19%)
  local copies, waits for them, and re-layouts  15.6 us (12%)
  other arithmetic  1.27 us (1%)
    ppermute x4, waiting for transfers between devices, hop(): return lax.ppermute(v, 'feat', pairs)  29.3 us
    ppermute x32, starting transfers between devices, swap(): return lax.ppermute(v, group, [(i, i ^ m) for i in range(size)])  27.5 us
    ppermute x32, waiting for transfers between devices, swap(): return lax.ppermute(v, group, [(i, i ^ m) for i in range(size)])  15.9 us
    unnamed x31, local copies, waits for them, and re-layouts  14.9 us
    pallas_call x3, Pallas kernels, project_call(): pl.pallas_call(functools.partial(project, chips), out_shape=[jax.ShapeDty...  12.6 us
    pallas_call x4, Pallas kernels, factor_call(): pl.pallas_call(functools.partial(factor_part, slots), out_shape=outs, gri...  10.3 us
    ppermute x4, starting transfers between devices, hop(): return lax.ppermute(v, 'feat', pairs)  10.1 us
  transfers between devices with their start and end apart: 36, of which 9 were waited for; matrix products, arithmetic and copies ran while one was open for 1% of the time, Pallas kernels for 17%

profile of v1, /device:TPU:0, one launch (start us, length us, event | category | flops | bytes accessed | tf_op | source)
XLA Modules:
  0.0 124.3 jit_solution(1023833785460065994)
XLA Ops:
  0.7 2.2 %copy-done = bf16[2048,1024]{1,0:T(8,128)(2,1)S(1)} copy-done((bf16[2048,1024]{1,0:T(8,128)(2,1)S(1)}, bf16[2048,1024]{1,0:T(8,128)(2,1)}, u32[]{:S(2)}) %copy-start) | copy-done | bytes 4194328
  2.9 2.2 %copy-done.1 = bf16[2048,1024]{1,0:T(8,128)(2,1)S(1)} copy-done((bf16[2048,1024]{1,0:T(8,128)(2,1)S(1)}, bf16[2048,1024]{1,0:T(8,128)(2,1)}, u32[]{:S(2)}) %copy-start.1) | copy-done | bytes 4194328
  7.5 2.4 %shard_map.76 = f32[2,1024,256]{2,1,0:T(8,128)S(1)} custom-call(s32[3]{0:T(128)S(1)} %dynamic-slice_bitcast_fusion.scal, bf16[2048,1024]{1,0:T(8,128)(2,1)S(1)} %copy-done, bf16[2048,1024]{1,0:T(8,128)(2,1)S(1)} %copy-done.1, bf16[1024,512]{1,0:T(8,128)(2,1)S(1)} %copy-done.2, bf16[1024,512]{1,0:T(8,128)(2,1)S(1)} %copy-done.2, ...), custom_call_target="tpu_custom_call" | custom-call | flops 1073741824 | bytes 7340032 | tf_op jit(solution)/shard_map/pallas_call | solution.py:78
  10.5 2.4 %shard_map.73 = f32[2,1024,256]{2,1,0:T(8,128)S(1)} custom-call(s32[3]{0:T(128)S(1)} %dynamic-slice_bitcast_fusion.scal, bf16[2048,1024]{1,0:T(8,128)(2,1)S(1)} %copy-done, bf16[2048,1024]{1,0:T(8,128)(2,1)S(1)} %copy-done.1, bf16[1024,512]{1,0:T(8,128)(2,1)S(1)} %copy-done.2, bf16[1024,512]{1,0:T(8,128)(2,1)S(1)} %copy-done.2, ...), custom_call_target="tpu_custom_call" | custom-call | flops 1073741824 | bytes 7340032 | tf_op jit(solution)/shard_map/pallas_call | solution.py:78
  14.2 2.8 %shard_map.77 = (f32[2,256,128]{2,1,0:T(8,128)S(1)}, f32[2,264,128]{2,1,0:T(8,128)S(1)}, f32[2,264,128]{2,1,0:T(8,128)S(1)}, f32[2,264,128]{2,1,0:T(8,128)S(1)},...) custom-call(s32[3]{0:T(128)S(1)} %dynamic-slice_bitcast_fusion.scal,, ...), custom_call_target="tpu_custom_call" | custom-call | flops 1073741824 | bytes 7340032 | tf_op jit(solution)/shard_map/pallas_call | solution.py:78
  17.1 2.9 %collective-permute-start.25 = (f16[2,264,128]{2,1,0:T(8,128)(2,1)S(1)}, f16[2,264,128]{2,1,0:T(8,128)(2,1)S(1)}, u32[]{:S(2)}, u32[]{:S(2)}) collective-permute-start(f16[2,264,128]{2,1,0:T(8,128)(2,1)S(1)} %convert_element_type.91), channel_id=1, source_target_pairs={{0,2},{1,3},{2,0},{3,1},{16,18},{17,19},{18,16},{19,17},{4,6},{5,7... | collective-permute-start | bytes 405512 | tf_op jit(solution)/shard_map/ppermute | solution.py:191
  20.0 1.6 %collective-permute-start.26 = (f16[2,264,128]{2,1,0:T(8,128)(2,1)S(1)}, f16[2,264,128]{2,1,0:T(8,128)(2,1)S(1)}, u32[]{:S(2)}, u32[]{:S(2)}) collective-permute-start(f16[2,264,128]{2,1,0:T(8,128)(2,1)S(1)} %convert_element_type.93), channel_id=1, source_target_pairs={{0,16},{1,17},{2,18},{3,19},{16,0},{17,1},{18,2},{19,3},{4,20},{5,... | collective-permute-start | bytes 405512 | tf_op jit(solution)/shard_map/ppermute | solution.py:191
  21.7 2.0 %collective-permute-start.12 = (f16[2,264,128]{2,1,0:T(8,128)(2,1)S(1)}, f16[2,264,128]{2,1,0:T(8,128)(2,1)S(1)}, u32[]{:S(2)}, u32[]{:S(2)}) collective-permute-start(f16[2,264,128]{2,1,0:T(8,128)(2,1)S(1)} %convert_element_type.84), channel_id=1, source_target_pairs={{0,2},{1,3},{2,0},{3,1},{16,18},{17,19},{18,16},{19,17},{4,6},{5,7... | collective-permute-start | bytes 405512 | tf_op jit(solution)/shard_map/ppermute | solution.py:191
  23.9 1.6 %collective-permute-start.13 = (f16[2,264,128]{2,1,0:T(8,128)(2,1)S(1)}, f16[2,264,128]{2,1,0:T(8,128)(2,1)S(1)}, u32[]{:S(2)}, u32[]{:S(2)}) collective-permute-start(f16[2,264,128]{2,1,0:T(8,128)(2,1)S(1)} %convert_element_type.86), channel_id=1, source_target_pairs={{0,16},{1,17},{2,18},{3,19},{16,0},{17,1},{18,2},{19,3},{4,20},{5,... | collective-permute-start | bytes 405512 | tf_op jit(solution)/shard_map/ppermute | solution.py:191
  25.4 2.8 %shard_map.74 = (f32[2,256,256]{2,1,0:T(8,128)S(1)}, f32[2,264,256]{2,1,0:T(8,128)S(1)}, f32[2,264,256]{2,1,0:T(8,128)S(1)}, f32[2,264,256]{2,1,0:T(8,128)S(1)}) custom-call(s32[3]{0:T(128)S(1)} %dynamic-slice_bitcast_fusion.scal, bf16[2048,1024]{1,0:T(8,128)(2,1)S(1)} %copy-done, bf16[2048,1024]{1,0:T(8,128)(2,1)S(1)} %copy-done.1, ...), custom_call_target="tpu_custom_call" | custom-call | flops 1073741824 | bytes 7340032 | tf_op jit(solution)/shard_map/pallas_call | solution.py:78
  28.5 3.0 %collective-permute-start.3 = (f16[2,264,256]{2,1,0:T(8,128)(2,1)S(1)}, f16[2,264,256]{2,1,0:T(8,128)(2,1)S(1)}, u32[]{:S(2)}, u32[]{:S(2)}) collective-permute-start(f16[2,264,256]{2,1,0:T(8,128)(2,1)S(1)} %convert_element_type.81), channel_id=1, source_target_pairs={{0,18},{1,19},{2,16},{3,17},{16,2},{17,3},{18,0},{19,1},{4,22},{5,... | collective-permute-start | bytes 811016 | tf_op jit(solution)/shard_map/ppermute | solution.py:191
  32.7 1.8 %collective-permute-start.28 = (bf16[2,256,128]{2,1,0:T(8,128)(2,1)S(1)}, bf16[2,256,128]{2,1,0:T(8,128)(2,1)S(1)}, u32[]{:S(2)}, u32[]{:S(2)}) collective-permute-start(bf16[2,256,128]{2,1,0:T(8,128)(2,1)S(1)} %fusion.5.rest_0_), channel_id=1, source_target_pairs={{0,2},{1,3},{2,0},{3,1},{16,18},{17,19},{18,16},{19,17},{4,6},{5,7... | collective-permute-start | bytes 393224 | tf_op jit(solution)/shard_map/ppermute | solution.py:191
  34.5 1.4 %collective-permute-done.14 = f16[2,264,128]{2,1,0:T(8,128)(2,1)S(1)} collective-permute-done((f16[2,264,128]{2,1,0:T(8,128)(2,1)S(1)}, f16[2,264,128]{2,1,0:T(8,128)(2,1)S(1)}, u32[]{:S(2)}, u32[]{:S(2)}) %collective-permute-start.14) | collective-permute-done | bytes 135200 | tf_op jit(solution)/shard_map/ppermute | solution.py:191
  36.9 4.7 %collective-permute-done.3 = f16[2,264,256]{2,1,0:T(8,128)(2,1)S(1)} collective-permute-done((f16[2,264,256]{2,1,0:T(8,128)(2,1)S(1)}, f16[2,264,256]{2,1,0:T(8,128)(2,1)S(1)}, u32[]{:S(2)}, u32[]{:S(2)}) %collective-permute-start.3) | collective-permute-done | bytes 270368 | tf_op jit(solution)/shard_map/ppermute | solution.py:191
  41.6 1.8 %collective-permute-start.30 = (bf16[2,256,128]{2,1,0:T(8,128)(2,1)S(1)}, bf16[2,256,128]{2,1,0:T(8,128)(2,1)S(1)}, u32[]{:S(2)}, u32[]{:S(2)}) collective-permute-start(bf16[2,256,128]{2,1,0:T(8,128)(2,1)S(1)} %fusion.5.rest_0_), channel_id=1, source_target_pairs={{0,18},{1,19},{2,16},{3,17},{16,2},{17,3},{18,0},{19,1},{4,22},{5,... | collective-permute-start | bytes 393224 | tf_op jit(solution)/shard_map/ppermute | solution.py:191
  43.5 3.3 %collective-permute-done.2 = f16[2,264,256]{2,1,0:T(8,128)(2,1)S(1)} collective-permute-done((f16[2,264,256]{2,1,0:T(8,128)(2,1)S(1)}, f16[2,264,256]{2,1,0:T(8,128)(2,1)S(1)}, u32[]{:S(2)}, u32[]{:S(2)}) %collective-permute-start.2) | collective-permute-done | bytes 270368 | tf_op jit(solution)/shard_map/ppermute | solution.py:191
  48.2 1.5 %collective-permute-done.28.rest_1_ = bf16[2,256,128]{2,1,0:T(8,128)(2,1)S(1)} collective-permute-done((bf16[2,256,128]{2,1,0:T(8,128)(2,1)S(1)}, bf16[2,256,128]{2,1,0:T(8,128)(2,1)S(1)}, u32[]{:S(2)}, u32[]{:S(2)}) %collective-permute-start.28) | collective-permute-done | bytes 131104 | tf_op jit(solution)/shard_map/ppermute | solution.py:191
  52.4 1.6 %collective-permute-done.15.rest_1_ = bf16[2,256,128]{2,1,0:T(8,128)(2,1)S(1)} collective-permute-done((bf16[2,256,128]{2,1,0:T(8,128)(2,1)S(1)}, bf16[2,256,128]{2,1,0:T(8,128)(2,1)S(1)}, u32[]{:S(2)}, u32[]{:S(2)}) %collective-permute-start.15) | collective-permute-done | bytes 131104 | tf_op jit(solution)/shard_map/ppermute | solution.py:191
  54.2 1.9 %collective-permute-done.16.rest_2_ = bf16[2,256,128]{2,1,0:T(8,128)(2,1)S(1)} collective-permute-done((bf16[2,256,128]{2,1,0:T(8,128)(2,1)S(1)}, bf16[2,256,128]{2,1,0:T(8,128)(2,1)S(1)}, u32[]{:S(2)}, u32[]{:S(2)}) %collective-permute-start.16) | collective-permute-done | bytes 131104 | tf_op jit(solution)/shard_map/ppermute | solution.py:191
  56.1 1.7 %collective-permute-start.6 = (bf16[2,256,256]{2,1,0:T(8,128)(2,1)S(1)}, bf16[2,256,256]{2,1,0:T(8,128)(2,1)S(1)}, u32[]{:S(2)}, u32[]{:S(2)}) collective-permute-start(bf16[2,256,256]{2,1,0:T(8,128)(2,1)S(1)} %fusion.1.rest_0_), channel_id=1, source_target_pairs={{0,18},{1,19},{2,16},{3,17},{16,2},{17,3},{18,0},{19,1},{4,22},{5,... | collective-permute-start | bytes 786440 | tf_op jit(solution)/shard_map/ppermute | solution.py:191
  59.5 1.6 %collective-permute-start.4 = (bf16[2,256,256]{2,1,0:T(8,128)(2,1)S(1)}, bf16[2,256,256]{2,1,0:T(8,128)(2,1)S(1)}, u32[]{:S(2)}, u32[]{:S(2)}) collective-permute-start(bf16[2,256,256]{2,1,0:T(8,128)(2,1)S(1)} %fusion.1.rest_0_), channel_id=1, source_target_pairs={{0,2},{1,3},{2,0},{3,1},{16,18},{17,19},{18,16},{19,17},{4,6},{5,7... | collective-permute-start | bytes 786440 | tf_op jit(solution)/shard_map/ppermute | solution.py:191
  62.4 4.2 %shard_map.78 = bf16[2,1280,128]{2,1,0:T(8,128)(2,1)S(1)} custom-call(s32[3]{0:T(128)S(1)} %dynamic-slice_bitcast_fusion.scal, bf16[1280,2048]{1,0:T(8,128)(2,1)S(1)} %bitcast.18, bf16[1280,2048]{1,0:T(8,128)(2,1)S(1)} %bitcast.20, bf16[2,256,128]{2,1,0:T(8,128)(2,1)S(1)} %fusion.9.rest_0_, bf16[2,256,128]{2,1,0:T(8,128)(2,1)S(1)} %collective-permute-done.15.rest_1_, ...), custom_call_target="tpu_custom_call" | custom-call | flops 1342177280 | bytes 11534336 | tf_op jit(solution)/shard_map/pallas_call | solution.py:130
  67.2 1.5 %collective-permute-start.22 = (bf16[2,1280,128]{2,1,0:T(8,128)(2,1)S(1)}, bf16[2,1280,128]{2,1,0:T(8,128)(2,1)}, u32[]{:S(2)}, u32[]{:S(2)}) collective-permute-start(bf16[2,1280,128]{2,1,0:T(8,128)(2,1)S(1)} %shard_map.78), channel_id=1, source_target_pairs={{12,8},{8,4},{13,9},{9,5},{14,10},{10,6},{15,11},{11,7},{28,24},{2... | collective-permute-start | bytes 1966088 | tf_op jit(solution)/shard_map/ppermute | solution.py:194
  68.7 4.1 %collective-permute-start.23 = (bf16[2,1280,128]{2,1,0:T(8,128)(2,1)S(1)}, bf16[2,1280,128]{2,1,0:T(8,128)(2,1)}, u32[]{:S(2)}, u32[]{:S(2)}) collective-permute-start(bf16[2,1280,128]{2,1,0:T(8,128)(2,1)S(1)} %shard_map.78), channel_id=1, source_target_pairs={{0,4},{4,8},{1,5},{5,9},{2,6},{6,10},{3,7},{7,11},{16,20},{20,24},... | collective-permute-start | bytes 1966088 | tf_op jit(solution)/shard_map/ppermute | solution.py:194
  73.6 2.5 %copy-done.4 = bf16[1280,2048]{1,0:T(8,128)(2,1)S(1)} copy-done((bf16[1280,2048]{1,0:T(8,128)(2,1)S(1)}, bf16[1280,2048]{1,0:T(8,128)(2,1)}, u32[]{:S(2)}) %copy-start.4) | copy-done | bytes 5242904
  76.1 2.5 %copy-done.5 = bf16[1280,2048]{1,0:T(8,128)(2,1)S(1)} copy-done((bf16[1280,2048]{1,0:T(8,128)(2,1)S(1)}, bf16[1280,2048]{1,0:T(8,128)(2,1)}, u32[]{:S(2)}) %copy-start.5) | copy-done | bytes 5242904
  80.4 4.2 %shard_map.79 = f32[2,1280,128]{2,1,0:T(8,128)S(1)} custom-call(s32[3]{0:T(128)S(1)} %dynamic-slice_bitcast_fusion.scal, bf16[1280,2048]{1,0:T(8,128)(2,1)S(1)} %copy-done.4, bf16[1280,2048]{1,0:T(8,128)(2,1)S(1)} %copy-done.5, bf16[2,256,128]{2,1,0:T(8,128)(2,1)S(1)} %fusion.5.rest_0_, bf16[2,256,128]{2,1,0:T(8,128)(2,1)S(1)} %collective-permute-done.28.rest_1_, ...), custom_call_target="tpu_custom_call" | custom-call | flops 1342177280 | bytes 11534336 | tf_op jit(solution)/shard_map/pallas_call | solution.py:130
  84.6 4.3 %shard_map.75 = (bf16[2,1280,128]{2,1,0:T(8,128)(2,1)S(1)}, f32[2,1280,128]{2,1,0:T(8,128)S(1)}) custom-call(s32[3]{0:T(128)S(1)} %dynamic-slice_bitcast_fusion.scal, bf16[1280,2048]{1,0:T(8,128)(2,1)S(1)} %copy-done.4, bf16[1280,2048]{1,0:T(8,128)(2,1)S(1)} %copy-done.5, bf16[2,256,256]{2,1,0:T(8,128)(2,1)S(1)} %fusion.1.rest_0_, ...), custom_call_target="tpu_custom_call" | custom-call | flops 2684354560 | bytes 12582912 | tf_op jit(solution)/shard_map/pallas_call | solution.py:130
  88.8 2.0 %collective-permute-start.24 = (bf16[2,1280,128]{2,1,0:T(8,128)(2,1)S(1)}, bf16[2,1280,128]{2,1,0:T(8,128)(2,1)S(1)}, u32[]{:S(2)}, u32[]{:S(2)}) collective-permute-start(bf16[2,1280,128]{2,1,0:T(8,128)(2,1)S(1)} %get-tuple-element.28), channel_id=1, source_target_pairs={{0,4},{4,0},{8,12},{12,8},{1,5},{5,1},{9,13},{13,9},{2,6},{6,2},{1... | collective-permute-start | bytes 1966088 | tf_op jit(solution)/shard_map/ppermute | solution.py:194
  91.2 2.5 %collective-permute-start.35 = (bf16[2,1280,128]{2,1,0:T(8,128)(2,1)S(1)}, bf16[2,1280,128]{2,1,0:T(8,128)(2,1)S(1)}, u32[]{:S(2)}, u32[]{:S(2)}) collective-permute-start(bf16[2,1280,128]{2,1,0:T(8,128)(2,1)S(1)} %add_convert_fusion), channel_id=1, source_target_pairs={{0,8},{4,12},{8,0},{12,4},{1,9},{5,13},{9,1},{13,5},{2,10},{6,14},... | collective-permute-start | bytes 1966088 | tf_op jit(solution)/shard_map/ppermute | solution.py:194
  93.7 24.4 %collective-permute-done.24.refs_2_ = bf16[2,1280,128]{2,1,0:T(8,128)(2,1)S(1)} collective-permute-done((bf16[2,1280,128]{2,1,0:T(8,128)(2,1)S(1)}, bf16[2,1280,128]{2,1,0:T(8,128)(2,1)S(1)}, u32[]{:S(2)}, u32[]{:S(2)}) %collective-permute-start.24) | collective-permute-done | bytes 655392 | tf_op jit(solution)/shard_map/ppermute | solution.py:194
  118.1 4.9 %collective-permute-done.35.refs_3_ = bf16[2,1280,128]{2,1,0:T(8,128)(2,1)S(1)} collective-permute-done((bf16[2,1280,128]{2,1,0:T(8,128)(2,1)S(1)}, bf16[2,1280,128]{2,1,0:T(8,128)(2,1)S(1)}, u32[]{:S(2)}, u32[]{:S(2)}) %collective-permute-start.35) | collective-permute-done | bytes 655392 | tf_op jit(solution)/shard_map/ppermute | solution.py:194
  (114 shorter events, 19.7 us)
Async XLA Ops:
  12.8 11.0 %collective-permute-start = (f32[2,1024,256]{2,1,0:T(8,128)S(1)}, f32[2,1024,256]{2,1,0:T(8,128)S(1)}, u32[]{:S(2)}, u32[]{:S(2)}) collective-permute-start(f32[2,1024,256]{2,1,0:T(8,128)S(1)} %shard_map.73), channel_id=1, source_target_pairs={{0,1},{1,0},{2,3},{3,2},{16,17},{17,16},{18,19},{19,18},{4,5},{5,4... | collective-permute-start | bytes 6291464 | tf_op jit(solution)/shard_map/ppermute | solution.py:191
  17.1 11.3 %collective-permute-start.25 = (f16[2,264,128]{2,1,0:T(8,128)(2,1)S(1)}, f16[2,264,128]{2,1,0:T(8,128)(2,1)S(1)}, u32[]{:S(2)}, u32[]{:S(2)}) collective-permute-start(f16[2,264,128]{2,1,0:T(8,128)(2,1)S(1)} %convert_element_type.91), channel_id=1, source_target_pairs={{0,2},{1,3},{2,0},{3,1},{16,18},{17,19},{18,16},{19,17},{4,6},{5,7... | collective-permute-start | bytes 405512 | tf_op jit(solution)/shard_map/ppermute | solution.py:191
  20.0 8.5 %collective-permute-start.26 = (f16[2,264,128]{2,1,0:T(8,128)(2,1)S(1)}, f16[2,264,128]{2,1,0:T(8,128)(2,1)S(1)}, u32[]{:S(2)}, u32[]{:S(2)}) collective-permute-start(f16[2,264,128]{2,1,0:T(8,128)(2,1)S(1)} %convert_element_type.93), channel_id=1, source_target_pairs={{0,16},{1,17},{2,18},{3,19},{16,0},{17,1},{18,2},{19,3},{4,20},{5,... | collective-permute-start | bytes 405512 | tf_op jit(solution)/shard_map/ppermute | solution.py:191
  21.6 9.9 %collective-permute-start.27 = (f16[2,264,128]{2,1,0:T(8,128)(2,1)S(1)}, f16[2,264,128]{2,1,0:T(8,128)(2,1)S(1)}, u32[]{:S(2)}, u32[]{:S(2)}) collective-permute-start(f16[2,264,128]{2,1,0:T(8,128)(2,1)S(1)} %convert_element_type.95), channel_id=1, source_target_pairs={{0,18},{1,19},{2,16},{3,17},{16,2},{17,3},{18,0},{19,1},{4,22},{5,... | collective-permute-start | bytes 405512 | tf_op jit(solution)/shard_map/ppermute | solution.py:191
  21.7 10.5 %collective-permute-start.12 = (f16[2,264,128]{2,1,0:T(8,128)(2,1)S(1)}, f16[2,264,128]{2,1,0:T(8,128)(2,1)S(1)}, u32[]{:S(2)}, u32[]{:S(2)}) collective-permute-start(f16[2,264,128]{2,1,0:T(8,128)(2,1)S(1)} %convert_element_type.84), channel_id=1, source_target_pairs={{0,2},{1,3},{2,0},{3,1},{16,18},{17,19},{18,16},{19,17},{4,6},{5,7... | collective-permute-start | bytes 405512 | tf_op jit(solution)/shard_map/ppermute | solution.py:191
  23.9 8.8 %collective-permute-start.13 = (f16[2,264,128]{2,1,0:T(8,128)(2,1)S(1)}, f16[2,264,128]{2,1,0:T(8,128)(2,1)S(1)}, u32[]{:S(2)}, u32[]{:S(2)}) collective-permute-start(f16[2,264,128]{2,1,0:T(8,128)(2,1)S(1)} %convert_element_type.86), channel_id=1, source_target_pairs={{0,16},{1,17},{2,18},{3,19},{16,0},{17,1},{18,2},{19,3},{4,20},{5,... | collective-permute-start | bytes 405512 | tf_op jit(solution)/shard_map/ppermute | solution.py:191
  28.4 7.5 %collective-permute-start.14 = (f16[2,264,128]{2,1,0:T(8,128)(2,1)S(1)}, f16[2,264,128]{2,1,0:T(8,128)(2,1)S(1)}, u32[]{:S(2)}, u32[]{:S(2)}) collective-permute-start(f16[2,264,128]{2,1,0:T(8,128)(2,1)S(1)} %convert_element_type.88), channel_id=1, source_target_pairs={{0,18},{1,19},{2,16},{3,17},{16,2},{17,3},{18,0},{19,1},{4,22},{5,... | collective-permute-start | bytes 405512 | tf_op jit(solution)/shard_map/ppermute | solution.py:191
  28.5 13.1 %collective-permute-start.3 = (f16[2,264,256]{2,1,0:T(8,128)(2,1)S(1)}, f16[2,264,256]{2,1,0:T(8,128)(2,1)S(1)}, u32[]{:S(2)}, u32[]{:S(2)}) collective-permute-start(f16[2,264,256]{2,1,0:T(8,128)(2,1)S(1)} %convert_element_type.81), channel_id=1, source_target_pairs={{0,18},{1,19},{2,16},{3,17},{16,2},{17,3},{18,0},{19,1},{4,22},{5,... | collective-permute-start | bytes 811016 | tf_op jit(solution)/shard_map/ppermute | solution.py:191
  31.5 15.4 %collective-permute-start.2 = (f16[2,264,256]{2,1,0:T(8,128)(2,1)S(1)}, f16[2,264,256]{2,1,0:T(8,128)(2,1)S(1)}, u32[]{:S(2)}, u32[]{:S(2)}) collective-permute-start(f16[2,264,256]{2,1,0:T(8,128)(2,1)S(1)} %convert_element_type.79), channel_id=1, source_target_pairs={{0,16},{1,17},{2,18},{3,19},{16,0},{17,1},{18,2},{19,3},{4,20},{5,... | collective-permute-start | bytes 811016 | tf_op jit(solution)/shard_map/ppermute | solution.py:191
  32.2 14.7 %collective-permute-start.1 = (f16[2,264,256]{2,1,0:T(8,128)(2,1)S(1)}, f16[2,264,256]{2,1,0:T(8,128)(2,1)S(1)}, u32[]{:S(2)}, u32[]{:S(2)}) collective-permute-start(f16[2,264,256]{2,1,0:T(8,128)(2,1)S(1)} %convert_element_type.77), channel_id=1, source_target_pairs={{0,2},{1,3},{2,0},{3,1},{16,18},{17,19},{18,16},{19,17},{4,6},{5,7... | collective-permute-start | bytes 811016 | tf_op jit(solution)/shard_map/ppermute | solution.py:191
  32.7 17.1 %collective-permute-start.28 = (bf16[2,256,128]{2,1,0:T(8,128)(2,1)S(1)}, bf16[2,256,128]{2,1,0:T(8,128)(2,1)S(1)}, u32[]{:S(2)}, u32[]{:S(2)}) collective-permute-start(bf16[2,256,128]{2,1,0:T(8,128)(2,1)S(1)} %fusion.5.rest_0_), channel_id=1, source_target_pairs={{0,2},{1,3},{2,0},{3,1},{16,18},{17,19},{18,16},{19,17},{4,6},{5,7... | collective-permute-start | bytes 393224 | tf_op jit(solution)/shard_map/ppermute | solution.py:191
  35.9 15.1 %collective-permute-start.29 = (bf16[2,256,128]{2,1,0:T(8,128)(2,1)S(1)}, bf16[2,256,128]{2,1,0:T(8,128)(2,1)S(1)}, u32[]{:S(2)}, u32[]{:S(2)}) collective-permute-start(bf16[2,256,128]{2,1,0:T(8,128)(2,1)S(1)} %fusion.5.rest_0_), channel_id=1, source_target_pairs={{0,16},{1,17},{2,18},{3,19},{16,0},{17,1},{18,2},{19,3},{4,20},{5,... | collective-permute-start | bytes 393224 | tf_op jit(solution)/shard_map/ppermute | solution.py:191
  41.6 10.2 %collective-permute-start.30 = (bf16[2,256,128]{2,1,0:T(8,128)(2,1)S(1)}, bf16[2,256,128]{2,1,0:T(8,128)(2,1)S(1)}, u32[]{:S(2)}, u32[]{:S(2)}) collective-permute-start(bf16[2,256,128]{2,1,0:T(8,128)(2,1)S(1)} %fusion.5.rest_0_), channel_id=1, source_target_pairs={{0,18},{1,19},{2,16},{3,17},{16,2},{17,3},{18,0},{19,1},{4,22},{5,... | collective-permute-start | bytes 393224 | tf_op jit(solution)/shard_map/ppermute | solution.py:191
  46.9 5.0 %collective-permute-start.31 = (bf16[2,256,128]{2,1,0:T(8,128)(2,1)S(1)}, bf16[2,256,128]{2,1,0:T(8,128)(2,1)S(1)}, u32[]{:S(2)}, u32[]{:S(2)}) collective-permute-start(bf16[2,256,128]{2,1,0:T(8,128)(2,1)S(1)} %fusion.5.rest_0_), channel_id=1, source_target_pairs={{0,1},{1,0},{2,3},{3,2},{16,17},{17,16},{18,19},{19,18},{4,5},{5,4... | collective-permute-start | bytes 393224 | tf_op jit(solution)/shard_map/ppermute | solution.py:191
  47.0 7.0 %collective-permute-start.15 = (bf16[2,256,128]{2,1,0:T(8,128)(2,1)S(1)}, bf16[2,256,128]{2,1,0:T(8,128)(2,1)S(1)}, u32[]{:S(2)}, u32[]{:S(2)}) collective-permute-start(bf16[2,256,128]{2,1,0:T(8,128)(2,1)S(1)} %fusion.9.rest_0_), channel_id=1, source_target_pairs={{0,2},{1,3},{2,0},{3,1},{16,18},{17,19},{18,16},{19,17},{4,6},{5,7... | collective-permute-start | bytes 393224 | tf_op jit(solution)/shard_map/ppermute | solution.py:191
  49.7 6.4 %collective-permute-start.16 = (bf16[2,256,128]{2,1,0:T(8,128)(2,1)S(1)}, bf16[2,256,128]{2,1,0:T(8,128)(2,1)S(1)}, u32[]{:S(2)}, u32[]{:S(2)}) collective-permute-start(bf16[2,256,128]{2,1,0:T(8,128)(2,1)S(1)} %fusion.9.rest_0_), channel_id=1, source_target_pairs={{0,16},{1,17},{2,18},{3,19},{16,0},{17,1},{18,2},{19,3},{4,20},{5,... | collective-permute-start | bytes 393224 | tf_op jit(solution)/shard_map/ppermute | solution.py:191
  51.0 6.8 %collective-permute-start.17 = (bf16[2,256,128]{2,1,0:T(8,128)(2,1)S(1)}, bf16[2,256,128]{2,1,0:T(8,128)(2,1)S(1)}, u32[]{:S(2)}, u32[]{:S(2)}) collective-permute-start(bf16[2,256,128]{2,1,0:T(8,128)(2,1)S(1)} %fusion.9.rest_0_), channel_id=1, source_target_pairs={{0,18},{1,19},{2,16},{3,17},{16,2},{17,3},{18,0},{19,1},{4,22},{5,... | collective-permute-start | bytes 393224 | tf_op jit(solution)/shard_map/ppermute | solution.py:191
  51.8 6.0 %collective-permute-start.18 = (bf16[2,256,128]{2,1,0:T(8,128)(2,1)S(1)}, bf16[2,256,128]{2,1,0:T(8,128)(2,1)S(1)}, u32[]{:S(2)}, u32[]{:S(2)}) collective-permute-start(bf16[2,256,128]{2,1,0:T(8,128)(2,1)S(1)} %fusion.9.rest_0_), channel_id=1, source_target_pairs={{0,1},{1,0},{2,3},{3,2},{16,17},{17,16},{18,19},{19,18},{4,5},{5,4... | collective-permute-start | bytes 393224 | tf_op jit(solution)/shard_map/ppermute | solution.py:191
  51.8 6.5 %collective-permute-start.32 = (bf16[2,256,128]{2,1,0:T(8,128)(2,1)S(1)}, bf16[2,256,128]{2,1,0:T(8,128)(2,1)S(1)}, u32[]{:S(2)}, u32[]{:S(2)}) collective-permute-start(bf16[2,256,128]{2,1,0:T(8,128)(2,1)S(1)} %collective-permute-done.28.rest_1_), channel_id=1, source_target_pairs={{0,1},{1,0},{2,3},{3,2},{16,17},{17,16},{18,19},{19,18},{4,5},{5,4... | collective-permute-start | bytes 393224 | tf_op jit(solution)/shard_map/ppermute | solution.py:191
  54.0 4.4 %collective-permute-start.33 = (bf16[2,256,128]{2,1,0:T(8,128)(2,1)S(1)}, bf16[2,256,128]{2,1,0:T(8,128)(2,1)S(1)}, u32[]{:S(2)}, u32[]{:S(2)}) collective-permute-start(bf16[2,256,128]{2,1,0:T(8,128)(2,1)S(1)} %collective-permute-done.29.rest_2_), channel_id=1, source_target_pairs={{0,1},{1,0},{2,3},{3,2},{16,17},{17,16},{18,19},{19,18},{4,5},{5,4... | collective-permute-start | bytes 393224 | tf_op jit(solution)/shard_map/ppermute | solution.py:191
  56.1 12.6 %collective-permute-start.6 = (bf16[2,256,256]{2,1,0:T(8,128)(2,1)S(1)}, bf16[2,256,256]{2,1,0:T(8,128)(2,1)S(1)}, u32[]{:S(2)}, u32[]{:S(2)}) collective-permute-start(bf16[2,256,256]{2,1,0:T(8,128)(2,1)S(1)} %fusion.1.rest_0_), channel_id=1, source_target_pairs={{0,18},{1,19},{2,16},{3,17},{16,2},{17,3},{18,0},{19,1},{4,22},{5,... | collective-permute-start | bytes 786440 | tf_op jit(solution)/shard_map/ppermute | solution.py:191
  59.0 7.5 %collective-permute-start.34 = (bf16[2,256,128]{2,1,0:T(8,128)(2,1)S(1)}, bf16[2,256,128]{2,1,0:T(8,128)(2,1)S(1)}, u32[]{:S(2)}, u32[]{:S(2)}) collective-permute-start(bf16[2,256,128]{2,1,0:T(8,128)(2,1)S(1)} %collective-permute-done.30.rest_3_), channel_id=1, source_target_pairs={{0,1},{1,0},{2,3},{3,2},{16,17},{17,16},{18,19},{19,18},{4,5},{5,4... | collective-permute-start | bytes 393224 | tf_op jit(solution)/shard_map/ppermute | solution.py:191
  59.5 13.4 %collective-permute-start.4 = (bf16[2,256,256]{2,1,0:T(8,128)(2,1)S(1)}, bf16[2,256,256]{2,1,0:T(8,128)(2,1)S(1)}, u32[]{:S(2)}, u32[]{:S(2)}) collective-permute-start(bf16[2,256,256]{2,1,0:T(8,128)(2,1)S(1)} %fusion.1.rest_0_), channel_id=1, source_target_pairs={{0,2},{1,3},{2,0},{3,1},{16,18},{17,19},{18,16},{19,17},{4,6},{5,7... | collective-permute-start | bytes 786440 | tf_op jit(solution)/shard_map/ppermute | solution.py:191
  61.1 12.0 %collective-permute-start.5 = (bf16[2,256,256]{2,1,0:T(8,128)(2,1)S(1)}, bf16[2,256,256]{2,1,0:T(8,128)(2,1)S(1)}, u32[]{:S(2)}, u32[]{:S(2)}) collective-permute-start(bf16[2,256,256]{2,1,0:T(8,128)(2,1)S(1)} %fusion.1.rest_0_), channel_id=1, source_target_pairs={{0,16},{1,17},{2,18},{3,19},{16,0},{17,1},{18,2},{19,3},{4,20},{5,... | collective-permute-start | bytes 786440 | tf_op jit(solution)/shard_map/ppermute | solution.py:191
  62.3 11.1 %collective-permute-start.7 = (bf16[2,256,256]{2,1,0:T(8,128)(2,1)S(1)}, bf16[2,256,256]{2,1,0:T(8,128)(2,1)S(1)}, u32[]{:S(2)}, u32[]{:S(2)}) collective-permute-start(bf16[2,256,256]{2,1,0:T(8,128)(2,1)S(1)} %fusion.1.rest_0_), channel_id=1, source_target_pairs={{0,1},{1,0},{2,3},{3,2},{16,17},{17,16},{18,19},{19,18},{4,5},{5,4... | collective-permute-start | bytes 786440 | tf_op jit(solution)/shard_map/ppermute | solution.py:191
  67.2 23.6 %collective-permute-start.22 = (bf16[2,1280,128]{2,1,0:T(8,128)(2,1)S(1)}, bf16[2,1280,128]{2,1,0:T(8,128)(2,1)}, u32[]{:S(2)}, u32[]{:S(2)}) collective-permute-start(bf16[2,1280,128]{2,1,0:T(8,128)(2,1)S(1)} %shard_map.78), channel_id=1, source_target_pairs={{12,8},{8,4},{13,9},{9,5},{14,10},{10,6},{15,11},{11,7},{28,24},{2... | collective-permute-start | bytes 1966088 | tf_op jit(solution)/shard_map/ppermute | solution.py:194
  68.7 22.1 %collective-permute-start.23 = (bf16[2,1280,128]{2,1,0:T(8,128)(2,1)S(1)}, bf16[2,1280,128]{2,1,0:T(8,128)(2,1)}, u32[]{:S(2)}, u32[]{:S(2)}) collective-permute-start(bf16[2,1280,128]{2,1,0:T(8,128)(2,1)S(1)} %shard_map.78), channel_id=1, source_target_pairs={{0,4},{4,8},{1,5},{5,9},{2,6},{6,10},{3,7},{7,11},{16,20},{20,24},... | collective-permute-start | bytes 1966088 | tf_op jit(solution)/shard_map/ppermute | solution.py:194
  72.9 11.7 %collective-permute-start.10 = (bf16[2,256,256]{2,1,0:T(8,128)(2,1)S(1)}, bf16[2,256,256]{2,1,0:T(8,128)(2,1)S(1)}, u32[]{:S(2)}, u32[]{:S(2)}) collective-permute-start(bf16[2,256,256]{2,1,0:T(8,128)(2,1)S(1)} %collective-permute-done.6.rest_3_), channel_id=1, source_target_pairs={{0,1},{1,0},{2,3},{3,2},{16,17},{17,16},{18,19},{19,18},{4,5},{5,4... | collective-permute-start | bytes 786440 | tf_op jit(solution)/shard_map/ppermute | solution.py:191
  73.1 11.5 %collective-permute-start.8 = (bf16[2,256,256]{2,1,0:T(8,128)(2,1)S(1)}, bf16[2,256,256]{2,1,0:T(8,128)(2,1)S(1)}, u32[]{:S(2)}, u32[]{:S(2)}) collective-permute-start(bf16[2,256,256]{2,1,0:T(8,128)(2,1)S(1)} %collective-permute-done.4.rest_1_), channel_id=1, source_target_pairs={{0,1},{1,0},{2,3},{3,2},{16,17},{17,16},{18,19},{19,18},{4,5},{5,4... | collective-permute-start | bytes 786440 | tf_op jit(solution)/shard_map/ppermute | solution.py:191
  73.4 11.2 %collective-permute-start.9 = (bf16[2,256,256]{2,1,0:T(8,128)(2,1)S(1)}, bf16[2,256,256]{2,1,0:T(8,128)(2,1)S(1)}, u32[]{:S(2)}, u32[]{:S(2)}) collective-permute-start(bf16[2,256,256]{2,1,0:T(8,128)(2,1)S(1)} %collective-permute-done.5.rest_2_), channel_id=1, source_target_pairs={{0,1},{1,0},{2,3},{3,2},{16,17},{17,16},{18,19},{19,18},{4,5},{5,4... | collective-permute-start | bytes 786440 | tf_op jit(solution)/shard_map/ppermute | solution.py:191
  88.8 29.3 %collective-permute-start.24 = (bf16[2,1280,128]{2,1,0:T(8,128)(2,1)S(1)}, bf16[2,1280,128]{2,1,0:T(8,128)(2,1)S(1)}, u32[]{:S(2)}, u32[]{:S(2)}) collective-permute-start(bf16[2,1280,128]{2,1,0:T(8,128)(2,1)S(1)} %get-tuple-element.28), channel_id=1, source_target_pairs={{0,4},{4,0},{8,12},{12,8},{1,5},{5,1},{9,13},{13,9},{2,6},{6,2},{1... | collective-permute-start | bytes 1966088 | tf_op jit(solution)/shard_map/ppermute | solution.py:194
  91.2 31.8 %collective-permute-start.35 = (bf16[2,1280,128]{2,1,0:T(8,128)(2,1)S(1)}, bf16[2,1280,128]{2,1,0:T(8,128)(2,1)S(1)}, u32[]{:S(2)}, u32[]{:S(2)}) collective-permute-start(bf16[2,1280,128]{2,1,0:T(8,128)(2,1)S(1)} %add_convert_fusion), channel_id=1, source_target_pairs={{0,8},{4,12},{8,0},{12,4},{1,9},{5,13},{9,1},{13,5},{2,10},{6,14},... | collective-permute-start | bytes 1966088 | tf_op jit(solution)/shard_map/ppermute | solution.py:194
  (18 other events, 182.4 us)
